TPU v7x, 32 devices: a whole 2x2x4 slice. The times are simulated.
32 devices in a mesh: grp: 2 (over y), win: 4 (over z), uly: 4 (over x, core).
Axes of the slice: x: 2, y: 2, z: 4, core: 2. Of those that a mesh axis runs over, the one named last changes fastest.
Arguments:
- query_rows: bfloat16 [8, 16, 64, 5120], P(('grp', 'win'), None, 'uly'), parts along dimension 0, may hold values from -140 to 140
- key_rows: bfloat16 [8, 16, 64, 5120], P(('grp', 'win'), None, 'uly'), parts along dimension 0, may hold values from -140 to 140
- value_rows: bfloat16 [8, 16, 64, 5120], P(('grp', 'win'), None, 'uly'), parts along dimension 0, may hold values from -6 to 6
- query_gain: float32 [5120], replicated, may hold values from 0.25 to 1.75
- key_gain: float32 [5120], replicated, may hold values from 0.25 to 1.75
- window_start: int32 [8], P('grp'), parts along dimension 0, may hold values from 0 to 40, as said below
- owner_of_phase: int32 [8], P('grp'), parts along dimension 0, may hold values from 0 to 3, each once
- blend_weight: int32 [8, 16], P('grp'), parts along dimension 0, may hold values from 1 to 8
Outputs:
- owned_frames: bfloat16 [96, 64, 5120], P(('grp', 'win'), 'uly'), parts along dimension 0
- next_windows: bfloat16 [8, 16, 64, 5120], P(('grp', 'win'), None, 'uly'), parts along dimension 0
There are 2 independent parts, one for each index of `grp`. A program takes and returns all parts, laid end to end along the dimension named above; an argument that names none is the same for every part. Nothing has to cross between parts.
Inputs may be any that keep to these rules, and one draw needn't show every extreme that they name: `window_start`: window w starts at frame w * 12 plus an offset of 0 to 4; in some pair of consecutive windows (the last one followed by the first counts as consecutive) the first offset is 4 and the second 0. `owner_of_phase`: a permutation.
All inputs are finite; a program needn't handle non-finite values.
Results may differ from a plain program's by a relative error of at most 0.0015.
The roundings to bfloat16 on the way count: a program that leaves them out, or rounds other values in their place, can miss the bound.
Values may be sent and summed in bfloat16 or wider, within the bound.
A program may use at most 128 MiB of HBM per device.

v0:
```python
import math

import jax
import jax.numpy as jnp
from jax import lax
from jax.sharding import PartitionSpec as P

HEADS = 40
WF = 16
FR = 12


def normalize(row_block, gain_vector):
    floats = row_block.astype(jnp.float32)
    mean_square = jnp.mean(floats * floats, axis=-1, keepdims=True)
    return (floats * lax.rsqrt(mean_square + 1e-06) * gain_vector).astype(jnp.bfloat16)


def head_attention(operands):
    query_head, key_head, value_head = operands
    scores = jnp.dot(query_head, key_head.T, preferred_element_type=jnp.float32) * (
        1.0 / math.sqrt(query_head.shape[-1])
    )
    row_max = jnp.max(scores, axis=-1, keepdims=True)
    exponent = jnp.exp(scores - row_max)
    weights = (exponent / jnp.sum(exponent, axis=-1, keepdims=True)).astype(jnp.bfloat16)
    return jnp.dot(weights, value_head, preferred_element_type=jnp.float32).astype(jnp.bfloat16)


def attend(operands):
    query_part, key_part, value_part = operands
    heads_here = query_part.shape[3]
    head_size = query_part.shape[4]
    token_count = query_part.shape[0] * query_part.shape[1]

    def flatten(tensor):
        return jnp.moveaxis(tensor.reshape(token_count, heads_here, head_size), 1, 0)

    result = lax.map(head_attention, (flatten(query_part), flatten(key_part), flatten(value_part)))
    return jnp.moveaxis(result, 0, 1).reshape(query_part.shape)


def table_lookup(table_row, wanted, length):
    entries = jnp.arange(length, dtype=jnp.int32)
    return jnp.sum(jnp.where(wanted[..., None] == entries, table_row, 0), axis=-1)


def send_owners(frame_rows, inverse, my_start, windows, capacity):
    slot_index = jnp.arange(capacity, dtype=jnp.int32)
    position_in = (inverse[:, None] - my_start) % windows + slot_index[None, :] * windows
    is_valid = (position_in < WF).reshape(-1)
    picked = jnp.take(frame_rows, jnp.minimum(position_in, WF - 1).reshape(-1), axis=0)
    picked = jnp.where(is_valid[:, None, None], picked, jnp.zeros_like(picked))
    packed = picked.reshape(windows, capacity, frame_rows.shape[1], frame_rows.shape[2])
    return lax.all_to_all(packed, "win", split_axis=0, concat_axis=0, tiled=True)


def combine_owned(received, window_start, blend_weight, my_phase, windows, frames_total, capacity):
    slot_index = jnp.arange(capacity, dtype=jnp.int32)
    source_pos = (my_phase - window_start[:, None]) % windows + slot_index[None, :] * windows
    arrived = source_pos < WF
    slot_at = (window_start[:, None] + source_pos) % frames_total // windows
    factor = table_lookup(blend_weight[:, None, :], source_pos, WF)
    owned_range = jnp.arange(FR, dtype=jnp.int32)
    mixing = jnp.where(
        (slot_at[None] == owned_range[:, None, None]) & arrived[None], factor[None], 0
    )
    mixing = mixing.reshape(FR, windows * capacity).astype(jnp.float32)
    numerator = jnp.dot(
        mixing.astype(jnp.bfloat16),
        received.reshape(windows * capacity, -1),
        preferred_element_type=jnp.float32,
    )
    denominator = jnp.sum(mixing, axis=1)
    owned = (numerator / denominator[:, None]).astype(jnp.bfloat16)
    return owned.reshape(FR, received.shape[2], received.shape[3])


def per_device(
    query_rows,
    key_rows,
    value_rows,
    query_gain,
    key_gain,
    window_start,
    owner_of_phase,
    blend_weight,
):
    windows = lax.axis_size("win")
    ulysses = lax.axis_size("uly")
    position = lax.axis_index("win")
    frames_total = FR * windows
    capacity = (WF + windows - 1) // windows
    shift_frames = FR // 2
    local_tokens = query_rows.shape[2]
    feature_count = query_rows.shape[3]
    groups = HEADS // ulysses
    head_size = feature_count // HEADS
    split_shape = (WF, local_tokens, ulysses, groups, head_size)
    query_heads = normalize(query_rows[0], query_gain).reshape(split_shape)
    key_heads = normalize(key_rows[0], key_gain).reshape(split_shape)
    value_heads = value_rows[0].reshape(split_shape)
    attended = attend(
        (
            lax.all_to_all(query_heads, "uly", split_axis=2, concat_axis=1, tiled=True),
            lax.all_to_all(key_heads, "uly", split_axis=2, concat_axis=1, tiled=True),
            lax.all_to_all(value_heads, "uly", split_axis=2, concat_axis=1, tiled=True),
        )
    )
    own_out = lax.all_to_all(attended, "uly", split_axis=1, concat_axis=2, tiled=True).reshape(
        WF, local_tokens, feature_count
    )
    phases = jnp.arange(windows, dtype=jnp.int32)
    inverse = jnp.sum(
        jnp.where(owner_of_phase[None, :] == phases[:, None], phases[None, :], 0), axis=1
    )
    my_start = window_start[position]
    my_phase = inverse[position]
    frame_range = jnp.arange(WF, dtype=jnp.int32)
    received = send_owners(own_out, inverse, my_start, windows, capacity)
    owned = combine_owned(
        received, window_start, blend_weight, my_phase, windows, frames_total, capacity
    )
    slot_index = jnp.arange(capacity, dtype=jnp.int32)
    target_pos = (my_phase - window_start[:, None] - shift_frames) % windows + slot_index[
        None, :
    ] * windows
    target_valid = (target_pos < WF).reshape(-1)
    target_slot = (
        (window_start[:, None] + shift_frames + target_pos) % frames_total // windows
    ).reshape(-1)
    outgoing = jnp.take(owned, target_slot, axis=0)
    outgoing = jnp.where(target_valid[:, None, None], outgoing, jnp.zeros_like(outgoing))
    outgoing = outgoing.reshape(windows, capacity, local_tokens, feature_count)
    returned = lax.all_to_all(outgoing, "win", split_axis=0, concat_axis=0, tiled=True)
    needed_phase = (my_start + shift_frames + frame_range) % windows
    source_owner = table_lookup(owner_of_phase[None, :], needed_phase, windows)
    flat_index = source_owner * capacity + frame_range // windows
    next_rows = jnp.take(
        returned.reshape(windows * capacity, local_tokens, feature_count), flat_index, axis=0
    )
    return (owned, next_rows[None])


def solution(mesh):
    placed = (
        P(("grp", "win"), None, "uly", None),
        P(("grp", "win"), None, "uly", None),
        P(("grp", "win"), None, "uly", None),
        P(),
        P(),
        P("grp"),
        P("grp"),
        P("grp", None),
    )
    return jax.shard_map(
        per_device,
        mesh=mesh,
        in_specs=placed,
        out_specs=(P(("grp", "win"), "uly", None), P(("grp", "win"), None, "uly", None)),
        check_vma=False,
    )
```

profile of v0, /device:TPU:0, one launch (start us, length us, event | category | flops | bytes accessed | tf_op | source)
XLA Modules:
  0.0 380.3 jit_solution(709549636202989451)
XLA Ops:
  0.6 6.8 %reshape.405 = f32[16,16,4,10,128]{4,3,2,1,0:T(8,128)} reshape(bf16[1,16,16,5120]{3,2,1,0:T(8,128)(2,1)} %param.13) | data formatting | bytes 7864320 | tf_op jit(solution)/shard_map/convert_element_type | solution.py:14
  8.2 4.0 %multiply_convert_fusion = bf16[16,16,4,10,128]{4,3,2,1,0:T(8,128)(2,1)S(1)} fusion(f32[16,16,4,10,128]{4,3,2,1,0:T(8,128)} %reshape.405, f32[4,10,128]{2,1,0:T(8,128)S(1)} %mul.80, f32[16,16]{1,0:T(8,128)S(1)} %add_rsqrt_fusion), kind=kLoop, calls=%fused_computation.23 | loop fusion | flops 3932160 | bytes 7885824 | tf_op jit(solution)/shard_map/convert_element_type | solution.py:16
  12.2 4.6 %copy.33 = bf16[16,16,4,10,128]{4,1,3,0,2:T(8,128)(2,1)} copy(bf16[16,16,4,10,128]{4,3,2,1,0:T(8,128)(2,1)S(1)} %multiply_convert_fusion) | data formatting | bytes 5242880 | tf_op jit(solution)/shard_map/convert_element_type | solution.py:16
  16.9 4.2 %all-to-all-start.1 = ((bf16[16,16,4,10,128]{4,1,3,0,2:T(8,128)(2,1)}), bf16[16,16,4,10,128]{4,1,3,0,2:T(8,128)(2,1)S(1)}, u32[]{:S(2)}, u32[]{:S(2)}) async-start(bf16[16,16,4,10,128]{4,1,3,0,2:T(8,128)(2,1)} %copy.33), calls=%async_computation.1 | async-start | bytes 5242880 | tf_op jit(solution)/shard_map/all_to_all | solution.py:106
  21.1 6.7 %reshape.404 = f32[16,16,4,10,128]{4,3,2,1,0:T(8,128)} reshape(bf16[1,16,16,5120]{3,2,1,0:T(8,128)(2,1)} %param.12) | data formatting | bytes 7864320 | tf_op jit(solution)/shard_map/convert_element_type | solution.py:14
  27.8 2.3 multiply_reduce_fusion.2
  30.1 4.1 %multiply_convert_fusion.1 = bf16[16,16,4,10,128]{4,3,2,1,0:T(8,128)(2,1)S(1)} fusion(f32[16,16,4,10,128]{4,3,2,1,0:T(8,128)} %reshape.404, f32[4,10,128]{2,1,0:T(8,128)S(1)} %mul.74, f32[16,16]{1,0:T(8,128)S(1)} %add_rsqrt_fusion.1), kind=kLoop, calls=%fused_computation.24 | loop fusion | flops 3932160 | bytes 7885824 | tf_op jit(solution)/shard_map/convert_element_type | solution.py:16
  34.2 4.5 %copy.31 = bf16[16,16,4,10,128]{4,1,3,0,2:T(8,128)(2,1)} copy(bf16[16,16,4,10,128]{4,3,2,1,0:T(8,128)(2,1)S(1)} %multiply_convert_fusion.1) | data formatting | bytes 5242880 | tf_op jit(solution)/shard_map/convert_element_type | solution.py:16
  38.7 13.7 %all-to-all-done.1 = bf16[16,16,4,10,128]{4,1,3,0,2:T(8,128)(2,1)S(1)} async-done(((bf16[16,16,4,10,128]{4,1,3,0,2:T(8,128)(2,1)}), bf16[16,16,4,10,128]{4,1,3,0,2:T(8,128)(2,1)S(1)}, u32[]{:S(2)}, u32[]{:S(2)}) %all-to-all-start.1) | async-done | bytes 2621472 | tf_op jit(solution)/shard_map/all_to_all | solution.py:106
  52.4 4.7 %all-to-all-start = ((bf16[16,16,4,10,128]{4,1,3,0,2:T(8,128)(2,1)}), bf16[16,16,4,10,128]{4,1,3,0,2:T(8,128)(2,1)}, u32[]{:S(2)}, u32[]{:S(2)}) async-start(bf16[16,16,4,10,128]{4,1,3,0,2:T(8,128)(2,1)} %copy.31), calls=%async_computation | async-start | bytes 5242880 | tf_op jit(solution)/shard_map/all_to_all | solution.py:105
  57.2 6.4 %reshape_squeeze.3 = bf16[16,16,4,10,128]{4,3,2,1,0:T(8,128)(2,1)} reshape(bf16[1,16,16,5120]{3,2,1,0:T(8,128)(2,1)} %param.14) | data formatting | bytes 5242880 | tf_op jit(solution)/shard_map/reshape;squeeze | solution.py:102
  63.5 6.7 %copy.35 = bf16[16,16,4,10,128]{4,1,3,0,2:T(8,128)(2,1)} copy(bf16[16,16,4,10,128]{4,3,2,1,0:T(8,128)(2,1)} %reshape_squeeze.3) | data formatting | bytes 5242880 | tf_op jit(solution)/shard_map/reshape;squeeze | solution.py:102
  70.2 18.1 %all-to-all-done = bf16[16,16,4,10,128]{4,1,3,0,2:T(8,128)(2,1)} async-done(((bf16[16,16,4,10,128]{4,1,3,0,2:T(8,128)(2,1)}), bf16[16,16,4,10,128]{4,1,3,0,2:T(8,128)(2,1)}, u32[]{:S(2)}, u32[]{:S(2)}) %all-to-all-start) | async-done | bytes 2621472 | tf_op jit(solution)/shard_map/all_to_all | solution.py:105
  88.3 4.5 %all-to-all-start.2 = ((bf16[16,16,4,10,128]{4,1,3,0,2:T(8,128)(2,1)}), bf16[16,16,4,10,128]{4,1,3,0,2:T(8,128)(2,1)}, u32[]{:S(2)}, u32[]{:S(2)}) async-start(bf16[16,16,4,10,128]{4,1,3,0,2:T(8,128)(2,1)} %copy.35), calls=%async_computation.2 | async-start | bytes 5242880 | tf_op jit(solution)/shard_map/all_to_all | solution.py:107
  92.9 2.3 copy.34
  95.2 2.5 copy.32
  97.7 26.5 %all-to-all-done.2 = bf16[16,16,4,10,128]{4,1,3,0,2:T(8,128)(2,1)} async-done(((bf16[16,16,4,10,128]{4,1,3,0,2:T(8,128)(2,1)}), bf16[16,16,4,10,128]{4,1,3,0,2:T(8,128)(2,1)}, u32[]{:S(2)}, u32[]{:S(2)}) %all-to-all-start.2) | async-done | bytes 2621472 | tf_op jit(solution)/shard_map/all_to_all | solution.py:107
  124.2 4.0 %copy.36 = bf16[16,16,4,10,128]{4,1,2,0,3:T(8,128)(2,1)} copy(bf16[16,16,4,10,128]{4,1,3,0,2:T(8,128)(2,1)} %all-to-all-done.2) | data formatting | bytes 5242880 | tf_op jit(solution)/shard_map/all_to_all | solution.py:107
  128.3 52.6 %while.10 = (s32[]{:T(128)}, bf16[10,1024,128]{2,1,0:T(8,128)(2,1)}, bf16[10,1024,128]{2,1,0:T(8,128)(2,1)S(1)}, bf16[10,1024,128]{2,1,0:T(8,128)(2,1)}, bf16[10,1024,128]{2,1,0:T(8,128)(2,1)}, /*index=5*/s32[]{:T(128)}) while((s32[]{:T(128)}, bf16[10,1024,128]{2,1,0:T(8,128)(2,1)}, bf16[10,1024,128]{2,1,0:T(8,128)(2,1)S(1)}, ...), condition=%wide.region_7.8_spmd, body=%wide.region_4.7_spmd.sunk | while | flops 546437120 | bytes 13654085 | solution.py:39
  130.7 2.8 fusion.37
  135.9 2.9 fusion.37
  138.8 1.7 multiply_reduce_fusion.4
  141.2 2.9 fusion.37
  144.0 1.7 multiply_reduce_fusion.4
  146.4 2.9 fusion.37
  151.7 2.9 fusion.37
  157.0 2.9 fusion.37
  162.2 2.9 fusion.37
  167.5 2.9 fusion.37
  170.4 1.7 multiply_reduce_fusion.4
  172.8 2.9 fusion.37
  175.7 1.7 multiply_reduce_fusion.4
  178.1 2.9 fusion.37
  180.9 4.9 %copy.37 = bf16[16,64,1,10,128]{4,0,3,2,1:T(8,128)(2,1)} copy(bf16[16,64,1,10,128]{4,1,0,3,2:T(8,128)(2,1)} %bitcast.19) | data formatting | bytes 5242880 | tf_op jit(solution)/shard_map/reshape | solution.py:40
  185.9 4.0 %all-to-all-start.3 = ((bf16[16,64,1,10,128]{4,0,3,2,1:T(8,128)(2,1)}), bf16[16,64,1,10,128]{4,0,3,2,1:T(8,128)(2,1)S(1)}, u32[]{:S(2)}, u32[]{:S(2)}) async-start(bf16[16,64,1,10,128]{4,0,3,2,1:T(8,128)(2,1)} %copy.37), calls=%async_computation.3 | async-start | bytes 5242880 | tf_op jit(solution)/shard_map/all_to_all | solution.py:110
  192.9 28.1 %all-to-all-done.3 = bf16[16,64,1,10,128]{4,0,3,2,1:T(8,128)(2,1)S(1)} async-done(((bf16[16,64,1,10,128]{4,0,3,2,1:T(8,128)(2,1)}), bf16[16,64,1,10,128]{4,0,3,2,1:T(8,128)(2,1)S(1)}, u32[]{:S(2)}, u32[]{:S(2)}) %all-to-all-start.3) | async-done | bytes 2621472 | tf_op jit(solution)/shard_map/all_to_all | solution.py:110
  221.9 4.3 %copy.39 = bf16[16,16,4,1,10,128]{5,4,2,1,0,3:T(8,128)(2,1)} copy(bf16[16,16,4,1,10,128]{5,1,2,4,0,3:T(8,128)(2,1)S(1)} %bitcast.83) | data formatting | bytes 5242880 | tf_op jit(solution)/shard_map/all_to_all | solution.py:110
  226.2 5.1 %reshape.399 = bf16[16,16,5120]{2,1,0:T(8,128)(2,1)S(1)} reshape(bf16[16,16,4,1,10,128]{5,4,2,1,0,3:T(8,128)(2,1)} %copy.39) | data formatting | bytes 5242880 | tf_op jit(solution)/shard_map/reshape | solution.py:110
  231.4 2.2 gather_fusion.1
  233.6 3.6 select_select_fusion
  237.2 5.9 %all-to-all-start.4 = ((bf16[4,4,16,5120]{3,2,1,0:T(8,128)(2,1)}), bf16[4,4,16,5120]{3,2,1,0:T(8,128)(2,1)S(1)}, u32[]{:S(2)}, u32[]{:S(2)}) async-start(bf16[4,4,16,5120]{3,2,1,0:T(8,128)(2,1)} %bitcast.81), calls=%async_computation.4 | async-start | bytes 5242880 | tf_op jit(solution)/shard_map/all_to_all | solution.py:55
  243.9 58.2 %all-to-all-done.4 = bf16[4,4,16,5120]{3,2,1,0:T(8,128)(2,1)S(1)} async-done(((bf16[4,4,16,5120]{3,2,1,0:T(8,128)(2,1)}), bf16[4,4,16,5120]{3,2,1,0:T(8,128)(2,1)S(1)}, u32[]{:S(2)}, u32[]{:S(2)}) %all-to-all-start.4) | async-done | bytes 2621472 | tf_op jit(solution)/shard_map/all_to_all | solution.py:55
  306.1 2.2 gather_fusion
  308.3 3.6 select_select_fusion.1
  311.9 3.7 all-to-all-start.5
  316.2 58.3 %all-to-all-done.5 = bf16[4,4,16,5120]{3,2,1,0:T(8,128)(2,1)S(1)} async-done(((bf16[4,4,16,5120]{3,2,1,0:T(8,128)(2,1)}), bf16[4,4,16,5120]{3,2,1,0:T(8,128)(2,1)S(1)}, u32[]{:S(2)}, u32[]{:S(2)}) %all-to-all-start.5) | async-done | bytes 2621472 | tf_op jit(solution)/shard_map/all_to_all | solution.py:135
  374.5 2.2 gather_fusion.2
  376.7 3.5 select_bitcast_fusion
  (69 shorter events, 26.9 us)
Async XLA Ops:
  0.6 6.8 %copy-start.1 = (bf16[1,16,16,5120]{3,2,1,0:T(8,128)(2,1)S(1)}, bf16[1,16,16,5120]{3,2,1,0:T(8,128)(2,1)}, u32[]{:S(2)}) copy-start(bf16[1,16,16,5120]{3,2,1,0:T(8,128)(2,1)} %param.13) | copy-start | bytes 7864324
  7.5 0.7 copy-start.2
  16.9 35.6 %all-to-all-start.1 = ((bf16[16,16,4,10,128]{4,1,3,0,2:T(8,128)(2,1)}), bf16[16,16,4,10,128]{4,1,3,0,2:T(8,128)(2,1)S(1)}, u32[]{:S(2)}, u32[]{:S(2)}) async-start(bf16[16,16,4,10,128]{4,1,3,0,2:T(8,128)(2,1)} %copy.33), calls=%async_computation.1 | async-start | bytes 5242880 | tf_op jit(solution)/shard_map/all_to_all | solution.py:106
  21.1 6.7 %copy-start.3 = (f32[5120]{0:T(1024)S(1)}, f32[5120]{0:T(1024)}, u32[]{:S(2)}) copy-start(f32[5120]{0:T(1024)} %param.15) | copy-start | bytes 61444
  52.4 35.9 %all-to-all-start = ((bf16[16,16,4,10,128]{4,1,3,0,2:T(8,128)(2,1)}), bf16[16,16,4,10,128]{4,1,3,0,2:T(8,128)(2,1)}, u32[]{:S(2)}, u32[]{:S(2)}) async-start(bf16[16,16,4,10,128]{4,1,3,0,2:T(8,128)(2,1)} %copy.31), calls=%async_computation | async-start | bytes 5242880 | tf_op jit(solution)/shard_map/all_to_all | solution.py:105
  88.3 35.9 %all-to-all-start.2 = ((bf16[16,16,4,10,128]{4,1,3,0,2:T(8,128)(2,1)}), bf16[16,16,4,10,128]{4,1,3,0,2:T(8,128)(2,1)}, u32[]{:S(2)}, u32[]{:S(2)}) async-start(bf16[16,16,4,10,128]{4,1,3,0,2:T(8,128)(2,1)} %copy.35), calls=%async_computation.2 | async-start | bytes 5242880 | tf_op jit(solution)/shard_map/all_to_all | solution.py:107
  185.9 4.0 %copy-start.6 = (s32[4]{0:T(128)S(1)}, s32[4]{0:T(128)}, u32[]{:S(2)}) copy-start(s32[4]{0:T(128)} %param.18) | copy-start | bytes 52
  185.9 4.7 %copy-start.5 = (s32[4]{0:T(128)S(1)}, s32[4]{0:T(128)}, u32[]{:S(2)}) copy-start(s32[4]{0:T(128)} %param.17) | copy-start | bytes 52
  185.9 35.0 %all-to-all-start.3 = ((bf16[16,64,1,10,128]{4,0,3,2,1:T(8,128)(2,1)}), bf16[16,64,1,10,128]{4,0,3,2,1:T(8,128)(2,1)S(1)}, u32[]{:S(2)}, u32[]{:S(2)}) async-start(bf16[16,64,1,10,128]{4,0,3,2,1:T(8,128)(2,1)} %copy.37), calls=%async_computation.3 | async-start | bytes 5242880 | tf_op jit(solution)/shard_map/all_to_all | solution.py:110
  237.1 6.0 %copy-start.4 = (s32[4,16]{1,0:T(4,128)S(1)}, s32[4,16]{1,0:T(4,128)}, u32[]{:S(2)}) copy-start(s32[4,16]{1,0:T(4,128)} %param.19) | copy-start | bytes 772
  237.2 65.0 %all-to-all-start.4 = ((bf16[4,4,16,5120]{3,2,1,0:T(8,128)(2,1)}), bf16[4,4,16,5120]{3,2,1,0:T(8,128)(2,1)S(1)}, u32[]{:S(2)}, u32[]{:S(2)}) async-start(bf16[4,4,16,5120]{3,2,1,0:T(8,128)(2,1)} %bitcast.81), calls=%async_computation.4 | async-start | bytes 5242880 | tf_op jit(solution)/shard_map/all_to_all | solution.py:55
  306.1 2.2 copy-start
  311.9 62.6 %all-to-all-start.5 = ((bf16[4,4,16,5120]{3,2,1,0:T(8,128)(2,1)}), bf16[4,4,16,5120]{3,2,1,0:T(8,128)(2,1)S(1)}, u32[]{:S(2)}, u32[]{:S(2)}) async-start(bf16[4,4,16,5120]{3,2,1,0:T(8,128)(2,1)} %select_select_fusion.1), calls=%async_computation.5 | async-start | bytes 5242880 | tf_op jit(solution)/shard_map/all_to_all | solution.py:135
where the time goes:
time: 382 us; the launch traced here: 380 us
  waiting for transfers between devices  203 us (53%)
  local copies, waits for them, and re-layouts  71.6 us (19%)
  matrix products  46.1 us (12%)
  other arithmetic  31.1 us (8%)
  starting transfers between devices  27.1 us (7%)
    all_to_all x1, waiting for transfers between devices, per_device(): lax.all_to_all(outgoing, 'win', split_axis=0, concat_axis=0, tiled=True)  58.3 us
    all_to_all x1, waiting for transfers between devices, send_owners(): lax.all_to_all(packed, 'win', split_axis=0, concat_axis=0, tiled=True)  58.2 us
    dot_general x10, matrix products, head_attention(): jnp.dot(weights, value_head, preferred_element_type=jnp.float32)  28.6 us
    all_to_all x1, waiting for transfers between devices, per_device(): lax.all_to_all(attended, 'uly', split_axis=1, concat_axis=2, tiled=True)  28.1 us
    all_to_all x1, waiting for transfers between devices, per_device(): lax.all_to_all(value_heads, 'uly', split_axis=2, concat_axis=1, tiled=True)  26.5 us
    all_to_all x1, waiting for transfers between devices, per_device(): lax.all_to_all(query_heads, 'uly', split_axis=2, concat_axis=1, tiled=True)  18.1 us
    dot_general x10, matrix products, head_attention(): jnp.dot(query_head, key_head.T, preferred_element_type=jnp.float32)  16.6 us
    all_to_all x1, waiting for transfers between devices, per_device(): lax.all_to_all(key_heads, 'uly', split_axis=2, concat_axis=1, tiled=True)  13.7 us
  transfers between devices with their start and end apart: 6, of which 6 were waited for; matrix products, arithmetic and copies ran while one was open for 10% of the time, Pallas kernels for 0%

commit v1 on v0

v1 whole, which is shorter than its diff:
```python
import functools
import math

import jax
import jax.numpy as jnp
from jax import lax
from jax.experimental import pallas as pl
from jax.experimental.pallas import tpu as pltpu
from jax.sharding import PartitionSpec as P

HEADS = 40
WF = 16
FR = 12
AHEAD = 2
LAG_BLEND = 1
LAG_RETURN = 2
LAG_LAST = 3
ROWS = 16


def fused(
    dims,
    send_pos,
    first_at,
    second_at,
    first_w,
    second_w,
    total_w,
    target_slot,
    next_at,
    q_ref,
    k_ref,
    v_ref,
    qg_ref,
    kg_ref,
    owned_ref,
    next_ref,
    stage,
    inbox,
    vbox,
    attended,
    z_out,
    z_in,
    x_out,
    x_in,
    r_out,
    r_in,
    z_now,
    x_now,
    qk_send,
    qk_recv,
    v_send,
    v_recv,
    zo_send,
    zo_recv,
    xo_send,
    xo_recv,
    ro_send,
    ro_recv,
):
    ulysses, windows, capacity, steps, head, tokens = dims
    local = tokens // WF
    me = lax.axis_index("uly")
    my_window = lax.axis_index("win")

    def peer(d):
        return lax.rem(me + d, ulysses)

    def far(d):
        return lax.rem(my_window + d, windows)

    barrier = pltpu.get_barrier_semaphore()
    for d in range(1, ulysses):
        pl.semaphore_signal(
            barrier, inc=1, device_id={"uly": peer(d)}, device_id_type=pl.DeviceIdType.MESH
        )
    for d in range(1, windows):
        pl.semaphore_signal(
            barrier, inc=1, device_id={"win": far(d)}, device_id_type=pl.DeviceIdType.MESH
        )
    pl.semaphore_wait(barrier, ulysses + windows - 2)

    def spread(source, target, send, recv, axis):
        mine = me if axis == "uly" else my_window
        count = ulysses if axis == "uly" else windows
        for d in range(1, count):
            to = lax.rem(mine + d, count)
            pltpu.make_async_remote_copy(
                src_ref=source(to),
                dst_ref=target(mine),
                send_sem=send,
                recv_sem=recv,
                device_id={axis: to},
                device_id_type=pl.DeviceIdType.MESH,
            ).start()
        pltpu.make_async_copy(source(mine), target(mine), recv).start()

    def arrived(ref, sem):
        pltpu.make_async_copy(ref, ref, sem).wait()

    def columns(u, s):
        return pl.ds(pl.multiple_of((u * steps + s) * head, head), head)

    def send_values(s):
        spread(
            lambda u: v_ref.at[:, columns(u, s)],
            lambda u: vbox.at[s, u],
            v_send.at[s],
            v_recv.at[s],
            "uly",
        )

    def send_scored(s):
        spread(
            lambda u: stage.at[u, s],
            lambda u: inbox.at[s, u],
            qk_send.at[s],
            qk_recv.at[s],
            "uly",
        )

    for s in range(AHEAD):
        send_values(s)

    def norm_block(t, carry):
        rows = pl.ds(pl.multiple_of(t * ROWS, ROWS), ROWS)
        for which, (ref, gain) in enumerate(((q_ref, qg_ref), (k_ref, kg_ref))):
            floats = ref[rows, :].astype(jnp.float32)
            mean_square = jnp.mean(floats * floats, axis=-1, keepdims=True)
            scaled = (floats * lax.rsqrt(mean_square + 1e-06) * gain[...]).astype(jnp.bfloat16)
            for u in range(ulysses):
                for s in range(steps):
                    at = (u * steps + s) * head
                    stage[u, s, which, rows, :] = scaled[:, at : at + head]
        return carry

    lax.fori_loop(0, tokens // ROWS, norm_block, 0)
    for s in range(AHEAD):
        send_scored(s)

    scale = 1.0 / math.sqrt(head)

    def attention(s):
        arrived(inbox.at[s], qk_recv.at[s])
        arrived(vbox.at[s], v_recv.at[s])

        @pl.when(s + AHEAD < steps)
        def _():
            send_scored(s + AHEAD)
            send_values(s + AHEAD)

        keys = inbox[s, :, 1].reshape(ulysses * tokens, head)
        values = vbox[s].reshape(ulysses * tokens, head)
        for u in range(ulysses):
            scores = (
                lax.dot_general(
                    inbox[s, u, 0],
                    keys,
                    (((1,), (1,)), ((), ())),
                    preferred_element_type=jnp.float32,
                )
                * scale
            )
            exponent = jnp.exp(scores - jnp.max(scores, axis=-1, keepdims=True))
            inverse_sum = 1.0 / jnp.sum(exponent, axis=-1, keepdims=True)
            weights = (exponent * inverse_sum).astype(jnp.bfloat16)
            result = jnp.dot(weights, values, preferred_element_type=jnp.float32)
            attended[:, u] = result.astype(jnp.bfloat16).reshape(WF, local, head)
        for o in range(windows):
            for c in range(capacity):
                z_out[s, o, c] = attended[send_pos[o * capacity + c]]
        spread(
            lambda o: z_out.at[s, o],
            lambda o: z_in.at[s, pl.ds(o * capacity, capacity)],
            zo_send.at[s],
            zo_recv.at[s],
            "win",
        )

    def blend(s):
        arrived(z_in.at[s], zo_recv.at[s])
        z_now[...] = z_in[s]
        for f in range(FR):
            numerator = first_w[f] * z_now[first_at[f]].astype(jnp.float32)
            numerator += second_w[f] * z_now[second_at[f]].astype(jnp.float32)
            x_out[s, :, f] = (numerator / total_w[f]).astype(jnp.bfloat16)
        spread(
            lambda u: x_out.at[s, u],
            lambda u: x_in.at[s, u],
            xo_send.at[s],
            xo_recv.at[s],
            "uly",
        )

    def give_back(s):
        arrived(x_in.at[s], xo_recv.at[s])
        x_now[...] = x_in[s]
        for o in range(windows):
            for c in range(capacity):
                r_out[s, o, c] = x_now[:, target_slot[o * capacity + c]]
        spread(
            lambda o: r_out.at[s, o],
            lambda o: r_in.at[s, pl.ds(o * capacity, capacity)],
            ro_send.at[s],
            ro_recv.at[s],
            "win",
        )
        for u in range(ulysses):
            owned_ref[:, :, columns(u, s)] = x_in[s, u]

    def finish(s):
        arrived(r_in.at[s], ro_recv.at[s])
        z_now[...] = r_in[s]
        for j in range(WF):
            frame = z_now[next_at[j]]
            for u in range(ulysses):
                next_ref[j, :, columns(u, s)] = frame[u]

    def step(i, carry):
        for lag, work in (
            (0, attention),
            (LAG_BLEND, blend),
            (LAG_RETURN, give_back),
            (LAG_LAST, finish),
        ):

            @pl.when((i >= lag) & (i < steps + lag))
            def _(lag=lag, work=work):
                work(i - lag)

        return carry

    lax.fori_loop(0, steps + LAG_LAST, step, 0)

    def sent(s, carry):
        arrived(inbox.at[s, pl.ds(0, ulysses - 1)], qk_send.at[s])
        arrived(vbox.at[s, pl.ds(0, ulysses - 1)], v_send.at[s])
        arrived(z_out.at[s, pl.ds(0, windows - 1)], zo_send.at[s])
        arrived(x_out.at[s, pl.ds(0, ulysses - 1)], xo_send.at[s])
        arrived(r_out.at[s, pl.ds(0, windows - 1)], ro_send.at[s])
        return carry

    lax.fori_loop(0, steps, sent, 0)


def per_device(
    query_rows,
    key_rows,
    value_rows,
    query_gain,
    key_gain,
    window_start,
    owner_of_phase,
    blend_weight,
):
    windows = lax.axis_size("win")
    ulysses = lax.axis_size("uly")
    position = lax.axis_index("win")
    frames_total = FR * windows
    capacity = (WF + windows - 1) // windows
    shift_frames = FR // 2
    local = query_rows.shape[2]
    features = query_rows.shape[3]
    head = features // HEADS
    steps = HEADS // ulysses
    tokens = WF * local

    phases = jnp.arange(windows, dtype=jnp.int32)
    inverse = jnp.sum(
        jnp.where(owner_of_phase[None, :] == phases[:, None], phases[None, :], 0), axis=1
    )
    my_start = window_start[position]
    my_phase = inverse[position]
    slots = jnp.arange(capacity, dtype=jnp.int32)
    send_pos = (inverse[:, None] - my_start) % windows + slots[None, :] * windows
    send_pos = jnp.minimum(send_pos, WF - 1).reshape(-1)

    frames = jnp.arange(FR, dtype=jnp.int32) * windows + my_phase
    offset = (frames[None, :] - window_start[:, None]) % frames_total
    holds = offset < WF
    factor = jnp.sum(
        jnp.where(
            offset[..., None] == jnp.arange(WF, dtype=jnp.int32), blend_weight[:, None, :], 0
        ),
        axis=-1,
    ).astype(jnp.float32)
    place = phases[:, None] * capacity + offset // windows
    first_window = jnp.min(jnp.where(holds, phases[:, None], windows), axis=0)
    last_window = jnp.max(jnp.where(holds, phases[:, None], -1), axis=0)
    is_first = phases[:, None] == first_window[None, :]
    is_last = phases[:, None] == last_window[None, :]
    is_other = is_last & ~is_first
    first_at = jnp.sum(jnp.where(is_first, place, 0), axis=0)
    second_at = jnp.sum(jnp.where(is_last, place, 0), axis=0)
    first_w = jnp.sum(jnp.where(is_first, factor, 0), axis=0)
    second_w = jnp.sum(jnp.where(is_other, factor, 0), axis=0)
    total_w = first_w + second_w

    target_pos = (my_phase - window_start[:, None] - shift_frames) % windows + slots[
        None, :
    ] * windows
    target_slot = (
        (window_start[:, None] + shift_frames + target_pos) % frames_total // windows
    ).reshape(-1)
    order = jnp.arange(WF, dtype=jnp.int32)
    needed = (my_start + shift_frames + order) % windows
    source = jnp.sum(jnp.where(needed[:, None] == phases[None, :], owner_of_phase[None, :], 0), 1)
    next_at = source * capacity + order // windows

    smem = pl.BlockSpec(memory_space=pltpu.SMEM)
    vmem = pl.BlockSpec(memory_space=pltpu.VMEM)
    bf16 = jnp.bfloat16
    sems = pltpu.SemaphoreType.DMA((steps,))
    frame = (ulysses, local, head)
    owned, next_rows = pl.pallas_call(
        functools.partial(fused, (ulysses, windows, capacity, steps, head, tokens)),
        out_shape=(
            jax.ShapeDtypeStruct((FR, local, features), bf16),
            jax.ShapeDtypeStruct((WF, local, features), bf16),
        ),
        in_specs=[smem] * 8 + [vmem] * 5,
        out_specs=(vmem, vmem),
        scratch_shapes=[
            pltpu.VMEM((ulysses, steps, 2, tokens, head), bf16),
            pltpu.VMEM((steps, ulysses, 2, tokens, head), bf16),
            pltpu.VMEM((steps, ulysses, tokens, head), bf16),
            pltpu.VMEM((WF,) + frame, bf16),
            pltpu.VMEM((steps, windows, capacity) + frame, bf16),
            pltpu.VMEM((steps, windows * capacity) + frame, bf16),
            pltpu.VMEM((steps, ulysses, FR, local, head), bf16),
            pltpu.VMEM((steps, ulysses, FR, local, head), bf16),
            pltpu.VMEM((steps, windows, capacity) + frame, bf16),
            pltpu.VMEM((steps, windows * capacity) + frame, bf16),
            pltpu.VMEM((windows * capacity,) + frame, bf16),
            pltpu.VMEM((ulysses, FR, local, head), bf16),
        ]
        + [sems] * 10,
        compiler_params=pltpu.CompilerParams(
            collective_id=0, has_side_effects=True, vmem_limit_bytes=66 * 1000 * 1000
        ),
    )(
        send_pos,
        first_at,
        second_at,
        first_w,
        second_w,
        total_w,
        target_slot,
        next_at,
        query_rows.reshape(tokens, features),
        key_rows.reshape(tokens, features),
        value_rows.reshape(tokens, features),
        query_gain.reshape(1, features),
        key_gain.reshape(1, features),
    )
    return (owned, next_rows[None])


def solution(mesh):
    placed = (
        P(("grp", "win"), None, "uly", None),
        P(("grp", "win"), None, "uly", None),
        P(("grp", "win"), None, "uly", None),
        P(),
        P(),
        P("grp"),
        P("grp"),
        P("grp", None),
    )
    return jax.shard_map(
        per_device,
        mesh=mesh,
        in_specs=placed,
        out_specs=(P(("grp", "win"), "uly", None), P(("grp", "win"), None, "uly", None)),
        check_vma=False,
    )
```

time: 382 us -> 164 us (0.43)
  waiting for transfers between devices: 203 us -> 0 us
  Pallas kernels: 0 us -> 146 us
  local copies, waits for them, and re-layouts: 71.6 us -> 7.1 us
  matrix products: 46.1 us -> 0 us
  starting transfers between devices: 27.1 us -> 0 us
  other arithmetic: 31.1 us -> 9.35 us
    all_to_all x6 -> x0, waiting for transfers between devices: 203 us -> none  [the longest x1 58.3 us: per_device(): lax.all_to_all(outgoing, 'win', split_axis=0, concat_axis=0, tiled=True)]
    pallas_call x0 -> x1, Pallas kernels: none -> 146 us  [per_device(): pl.pallas_call(functools.partial(fused, (ulysses, windows, capacity, step...]
    dot_general x21 -> x0, matrix products: 46.1 us -> none  [the longest x10 28.6 us: head_attention(): jnp.dot(weights, value_head, preferred_element_type=jnp.float32)]
    all_to_all x6 -> x0, starting transfers between devices: 27.1 us -> none  [the longest x1 5.89 us: send_owners(): lax.all_to_all(packed, 'win', split_axis=0, concat_axis=0, tiled=True)]
    convert_element_type x4 -> x0, local copies, waits for them, and re-layouts: 22.6 us -> none  [the longest x2 13.5 us: normalize(): floats = row_block.astype(jnp.float32)]
    all_to_all x5 -> x0, local copies, waits for them, and re-layouts: 14.1 us -> none  [the longest x2 5.28 us: per_device(): lax.all_to_all(attended, 'uly', split_axis=1, concat_axis=2, tiled=True)]
    another operation x2 -> x0, local copies, waits for them, and re-layouts: 13 us -> none  [per_device(): value_heads = value_rows[0].reshape(split_shape)]
    reshape x3 -> x0, local copies, waits for them, and re-layouts: 10.2 us -> none  [the longest x1 5.15 us: per_device(): lax.all_to_all(attended, 'uly', split_axis=1, concat_axis=2, tiled=True)]
  transfers between devices with their start and end apart: 6 -> 0, of which waited for: 6 -> 0; matrix products, arithmetic and copies ran while one was open for 10% -> 0% of each run, Pallas kernels for 0% -> 0%
where the time goes in v1:
time: 164 us
  Pallas kernels  146 us (89%)
  other arithmetic  9.35 us (6%)
  local copies, waits for them, and re-layouts  7.1 us (4%)
    pallas_call x1, Pallas kernels, per_device(): pl.pallas_call(functools.partial(fused, (ulysses, windows, capacity, step...  146 us
    unnamed x8, local copies, waits for them, and re-layouts  4.6 us

profile of v1, /device:TPU:0, one launch (start us, length us, event | category | flops | bytes accessed | tf_op | source)
XLA Modules:
  0.0 163.6 jit_solution(16189370729931156909)
XLA Ops:
  0.6 1.2 dynamic_slice.6
  2.5 0.7 select_reduce_fusion.7
  3.3 0.5 fusion.8.next_at
  3.8 0.8 select_reduce_fusion.8
  4.6 0.6 dynamic_slice.7
  5.2 0.7 and_select_fusion.5
  5.8 0.7 multiply_add_fusion
  6.5 1.3 broadcast_add_fusion
  7.8 0.8 select_reduce_fusion.4
  8.7 0.1 add_remainder_fusion
  8.7 0.1 rem.149
  8.8 0.6 and_select_fusion.2.target_slot
  9.4 0.6 min.8.send_pos
  10.0 1.4 select_reduce_fusion.3
  11.4 1.0 select_reduce_fusion
  12.4 0.2 select_reduce_fusion.1
  12.6 0.0 copy-start.1
  12.6 0.0 copy-start.2
  12.6 0.6 add.144.total_w
  13.2 0.0 copy-done.1
  13.2 0.0 copy-done.2
  13.2 145.8 %shard_map.95 = (bf16[12,16,5120]{2,1,0:T(8,128)(2,1)}, bf16[16,16,5120]{2,1,0:T(8,128)(2,1)}) custom-call(s32[16]{0:T(128)} %min.8.send_pos, s32[12]{0:T(128)} %get-tuple-element.9.first_at, s32[12]{0:T(128)} %get-tuple-element.8.second_at, f32[12]{0:T(128)} %copy-done.2, f32[12]{0:T(128)} %copy-done.1, f32[12]{0:T(128)} %add.144.total_w, ...), custom_call_target="tpu_custom_call" | custom-call | tf_op jit(solution)/shard_map/pallas_call | solution.py:315
  159.0 0.0 copy-start
  159.0 3.1 %copy.24 = bf16[12,16,5120]{2,1,0:T(8,128)(2,1)} copy(bf16[12,16,5120]{2,1,0:T(8,128)(2,1)} %get-tuple-element.21) | data formatting | bytes 3932160
  162.1 0.0 copy-done
  162.1 1.5 copy.25
  (1 shorter events, 0.0 us)
Async XLA Ops:
  12.6 0.6 copy-start.1
  12.6 0.6 copy-start.2
  159.0 3.1 %copy-start = (bf16[16,16,5120]{2,1,0:T(8,128)(2,1)S(1)}, bf16[16,16,5120]{2,1,0:T(8,128)(2,1)}, u32[]{:S(2)}) copy-start(bf16[16,16,5120]{2,1,0:T(8,128)(2,1)} %get-tuple-element.5) | copy-start | bytes 7864324

commit v2 on v1

--- a/solution.py
+++ b/solution.py
@@ -20,14 +20,9 @@
 
 def fused(
     dims,
-    send_pos,
-    first_at,
-    second_at,
-    first_w,
-    second_w,
-    total_w,
-    target_slot,
-    next_at,
+    start_ref,
+    owner_ref,
+    weight_ref,
     q_ref,
     k_ref,
     v_ref,
@@ -47,8 +42,18 @@
     r_in,
     z_now,
     x_now,
-    qk_send,
-    qk_recv,
+    inverse,
+    send_pos,
+    first_at,
+    second_at,
+    first_w,
+    second_w,
+    target_slot,
+    next_at,
+    q_send,
+    q_recv,
+    k_send,
+    k_recv,
     v_send,
     v_recv,
     zo_send,
@@ -110,51 +115,99 @@
             "uly",
         )
 
-    def send_scored(s):
-        spread(
-            lambda u: stage.at[u, s],
-            lambda u: inbox.at[s, u],
-            qk_send.at[s],
-            qk_recv.at[s],
+    def send_scored(which, s):
+        spread(
+            lambda u: stage.at[which, u, s],
+            lambda u: inbox.at[which, s, u],
+            (q_send, k_send)[which].at[s],
+            (q_recv, k_recv)[which].at[s],
             "uly",
         )
 
     for s in range(AHEAD):
         send_values(s)
 
-    def norm_block(t, carry):
-        rows = pl.ds(pl.multiple_of(t * ROWS, ROWS), ROWS)
-        for which, (ref, gain) in enumerate(((q_ref, qg_ref), (k_ref, kg_ref))):
+    frames_total = FR * windows
+    shift = FR // 2
+
+    def tables():
+        my_start = start_ref[my_window]
+
+        def invert(o, carry):
+            def seek(phase, found):
+                return jnp.where(owner_ref[phase] == o, phase, found)
+
+            inverse[o] = lax.fori_loop(0, windows, seek, jnp.int32(0))
+            return carry
+
+        lax.fori_loop(0, windows, invert, 0)
+        my_phase = inverse[my_window]
+
+        def per_window(o, carry):
+            for c in range(capacity):
+                ahead = lax.rem(inverse[o] - my_start + frames_total, windows) + c * windows
+                send_pos[o * capacity + c] = jnp.minimum(ahead, WF - 1)
+                base = start_ref[o] + shift
+                wanted = lax.rem(my_phase - base + 2 * frames_total, windows) + c * windows
+                target_slot[o * capacity + c] = lax.rem(base + wanted, frames_total) // windows
+            return carry
+
+        lax.fori_loop(0, windows, per_window, 0)
+
+        for f in range(FR):
+            frame = f * windows + my_phase
+            home = frame // FR
+            before = lax.rem(home + windows - 1, windows)
+            weight, place = [], []
+            for w in (home, before):
+                offset = lax.rem(frame - start_ref[w] + frames_total, frames_total)
+                held = jnp.minimum(offset, WF - 1)
+                weight.append(jnp.where(offset < WF, weight_ref[w, held], 0).astype(jnp.float32))
+                place.append(w * capacity + held // windows)
+            first_w[f], second_w[f] = weight
+            first_at[f], second_at[f] = place
+        for j in range(WF):
+            needed = lax.rem(my_start + shift + j, windows)
+            next_at[j] = owner_ref[needed] * capacity + j // windows
+
+    for which, (ref, gain) in enumerate(((q_ref, qg_ref), (k_ref, kg_ref))):
+
+        def norm_block(t, carry, which=which, ref=ref, gain=gain):
+            rows = pl.ds(pl.multiple_of(t * ROWS, ROWS), ROWS)
             floats = ref[rows, :].astype(jnp.float32)
             mean_square = jnp.mean(floats * floats, axis=-1, keepdims=True)
             scaled = (floats * lax.rsqrt(mean_square + 1e-06) * gain[...]).astype(jnp.bfloat16)
             for u in range(ulysses):
                 for s in range(steps):
                     at = (u * steps + s) * head
-                    stage[u, s, which, rows, :] = scaled[:, at : at + head]
-        return carry
-
-    lax.fori_loop(0, tokens // ROWS, norm_block, 0)
-    for s in range(AHEAD):
-        send_scored(s)
+                    stage[which, u, s, rows, :] = scaled[:, at : at + head]
+            return carry
+
+        lax.fori_loop(0, tokens // ROWS, norm_block, 0)
+        for s in range(AHEAD):
+            send_scored(which, s)
+
+    tables()
 
     scale = 1.0 / math.sqrt(head)
 
     def attention(s):
-        arrived(inbox.at[s], qk_recv.at[s])
+        arrived(inbox.at[0, s], q_recv.at[s])
+        arrived(inbox.at[1, s], k_recv.at[s])
         arrived(vbox.at[s], v_recv.at[s])
 
         @pl.when(s + AHEAD < steps)
         def _():
-            send_scored(s + AHEAD)
+            send_scored(0, s + AHEAD)
+            send_scored(1, s + AHEAD)
             send_values(s + AHEAD)
 
-        keys = inbox[s, :, 1].reshape(ulysses * tokens, head)
+        keys = inbox[1, s].reshape(ulysses * tokens, head)
         values = vbox[s].reshape(ulysses * tokens, head)
         for u in range(ulysses):
             scores = (
                 lax.dot_general(
-                    inbox[s, u, 0],
+                    inbox[0, s, u],
                     keys,
                     (((1,), (1,)), ((), ())),
                     preferred_element_type=jnp.float32,
@@ -183,7 +236,7 @@
         for f in range(FR):
             numerator = first_w[f] * z_now[first_at[f]].astype(jnp.float32)
             numerator += second_w[f] * z_now[second_at[f]].astype(jnp.float32)
-            x_out[s, :, f] = (numerator / total_w[f]).astype(jnp.bfloat16)
+            x_out[s, :, f] = (numerator / (first_w[f] + second_w[f])).astype(jnp.bfloat16)
         spread(
             lambda u: x_out.at[s, u],
             lambda u: x_in.at[s, u],
@@ -233,7 +286,8 @@
     lax.fori_loop(0, steps + LAG_LAST, step, 0)
 
     def sent(s, carry):
-        arrived(inbox.at[s, pl.ds(0, ulysses - 1)], qk_send.at[s])
+        arrived(inbox.at[0, s, pl.ds(0, ulysses - 1)], q_send.at[s])
+        arrived(inbox.at[1, s, pl.ds(0, ulysses - 1)], k_send.at[s])
         arrived(vbox.at[s, pl.ds(0, ulysses - 1)], v_send.at[s])
         arrived(z_out.at[s, pl.ds(0, windows - 1)], zo_send.at[s])
         arrived(x_out.at[s, pl.ds(0, ulysses - 1)], xo_send.at[s])
@@ -255,58 +309,12 @@
 ):
     windows = lax.axis_size("win")
     ulysses = lax.axis_size("uly")
-    position = lax.axis_index("win")
-    frames_total = FR * windows
     capacity = (WF + windows - 1) // windows
-    shift_frames = FR // 2
     local = query_rows.shape[2]
     features = query_rows.shape[3]
     head = features // HEADS
     steps = HEADS // ulysses
     tokens = WF * local
-
-    phases = jnp.arange(windows, dtype=jnp.int32)
-    inverse = jnp.sum(
-        jnp.where(owner_of_phase[None, :] == phases[:, None], phases[None, :], 0), axis=1
-    )
-    my_start = window_start[position]
-    my_phase = inverse[position]
-    slots = jnp.arange(capacity, dtype=jnp.int32)
-    send_pos = (inverse[:, None] - my_start) % windows + slots[None, :] * windows
-    send_pos = jnp.minimum(send_pos, WF - 1).reshape(-1)
-
-    frames = jnp.arange(FR, dtype=jnp.int32) * windows + my_phase
-    offset = (frames[None, :] - window_start[:, None]) % frames_total
-    holds = offset < WF
-    factor = jnp.sum(
-        jnp.where(
-            offset[..., None] == jnp.arange(WF, dtype=jnp.int32), blend_weight[:, None, :], 0
-        ),
-        axis=-1,
-    ).astype(jnp.float32)
-    place = phases[:, None] * capacity + offset // windows
-    first_window = jnp.min(jnp.where(holds, phases[:, None], windows), axis=0)
-    last_window = jnp.max(jnp.where(holds, phases[:, None], -1), axis=0)
-    is_first = phases[:, None] == first_window[None, :]
-    is_last = phases[:, None] == last_window[None, :]
-    is_other = is_last & ~is_first
-    first_at = jnp.sum(jnp.where(is_first, place, 0), axis=0)
-    second_at = jnp.sum(jnp.where(is_last, place, 0), axis=0)
-    first_w = jnp.sum(jnp.where(is_first, factor, 0), axis=0)
-    second_w = jnp.sum(jnp.where(is_other, factor, 0), axis=0)
-    total_w = first_w + second_w
-
-    target_pos = (my_phase - window_start[:, None] - shift_frames) % windows + slots[
-        None, :
-    ] * windows
-    target_slot = (
-        (window_start[:, None] + shift_frames + target_pos) % frames_total // windows
-    ).reshape(-1)
-    order = jnp.arange(WF, dtype=jnp.int32)
-    needed = (my_start + shift_frames + order) % windows
-    source = jnp.sum(jnp.where(needed[:, None] == phases[None, :], owner_of_phase[None, :], 0), 1)
-    next_at = source * capacity + order // windows
-
     smem = pl.BlockSpec(memory_space=pltpu.SMEM)
     vmem = pl.BlockSpec(memory_space=pltpu.VMEM)
     bf16 = jnp.bfloat16
@@ -318,11 +326,11 @@
             jax.ShapeDtypeStruct((FR, local, features), bf16),
             jax.ShapeDtypeStruct((WF, local, features), bf16),
         ),
-        in_specs=[smem] * 8 + [vmem] * 5,
+        in_specs=[smem] * 3 + [vmem] * 5,
         out_specs=(vmem, vmem),
         scratch_shapes=[
-            pltpu.VMEM((ulysses, steps, 2, tokens, head), bf16),
-            pltpu.VMEM((steps, ulysses, 2, tokens, head), bf16),
+            pltpu.VMEM((2, ulysses, steps, tokens, head), bf16),
+            pltpu.VMEM((2, steps, ulysses, tokens, head), bf16),
             pltpu.VMEM((steps, ulysses, tokens, head), bf16),
             pltpu.VMEM((WF,) + frame, bf16),
             pltpu.VMEM((steps, windows, capacity) + frame, bf16),
@@ -333,20 +341,23 @@
             pltpu.VMEM((steps, windows * capacity) + frame, bf16),
             pltpu.VMEM((windows * capacity,) + frame, bf16),
             pltpu.VMEM((ulysses, FR, local, head), bf16),
+            pltpu.SMEM((windows,), jnp.int32),
+            pltpu.SMEM((windows * capacity,), jnp.int32),
+            pltpu.SMEM((FR,), jnp.int32),
+            pltpu.SMEM((FR,), jnp.int32),
+            pltpu.SMEM((FR,), jnp.float32),
+            pltpu.SMEM((FR,), jnp.float32),
+            pltpu.SMEM((windows * capacity,), jnp.int32),
+            pltpu.SMEM((WF,), jnp.int32),
         ]
-        + [sems] * 10,
+        + [sems] * 12,
         compiler_params=pltpu.CompilerParams(
             collective_id=0, has_side_effects=True, vmem_limit_bytes=66 * 1000 * 1000
         ),
     )(
-        send_pos,
-        first_at,
-        second_at,
-        first_w,
-        second_w,
-        total_w,
-        target_slot,
-        next_at,
+        window_start,
+        owner_of_phase,
+        blend_weight,
         query_rows.reshape(tokens, features),
         key_rows.reshape(tokens, features),
         value_rows.reshape(tokens, features),

time: 164 us -> 150 us (0.915)
  other arithmetic: 9.35 us -> 0 us
  local copies, waits for them, and re-layouts: 7.1 us -> 4.59 us
    reduce_sum x5 -> x0, other arithmetic: 4.09 us -> none  [the longest x1 1.37 us: per_device(): second_at = jnp.sum(jnp.where(is_last, place, 0), axis=0)]
    add x4 -> x0, other arithmetic: 3.07 us -> none  [the longest x1 1.31 us: per_device(): window_start[:, None] + shift_frames + target_pos]
    dynamic_slice x2 -> x0, local copies, waits for them, and re-layouts: 1.83 us -> none  [the longest x1 1.24 us: per_device(): my_start = window_start[position]]
    unnamed x8 -> x4, local copies, waits for them, and re-layouts: 4.6 us -> 4.59 us
where the time goes in v2:
time: 150 us
  Pallas kernels  145 us (97%)
  local copies, waits for them, and re-layouts  4.59 us (3%)
    pallas_call x1, Pallas kernels, per_device(): pl.pallas_call(functools.partial(fused, (ulysses, windows, capacity, step...  145 us
    unnamed x4, local copies, waits for them, and re-layouts  4.59 us

profile of v2, /device:TPU:0, one launch (start us, length us, event | category | flops | bytes accessed | tf_op | source)
XLA Modules:
  0.0 149.8 jit_solution(6324855939536775662)
XLA Ops:
  0.6 144.6 %shard_map.95 = (bf16[12,16,5120]{2,1,0:T(8,128)(2,1)}, bf16[16,16,5120]{2,1,0:T(8,128)(2,1)}) custom-call(s32[4]{0:T(128)} %start_ref.1, s32[4]{0:T(128)} %owner_ref.1, s32[4,16]{1,0:T(4,128)} %weight_ref.1, bf16[256,5120]{1,0:T(8,128)(2,1)} %bitcast.6, bf16[256,5120]{1,0:T(8,128)(2,1)} %bitcast.7, bf16[256,5120]{1,0:T(8,128)(2,1)} %bitcast.8, ...), custom_call_target="tpu_custom_call" | custom-call | tf_op jit(solution)/shard_map/pallas_call | solution.py:323
  145.2 0.0 copy-start
  145.2 3.1 %copy.12 = bf16[12,16,5120]{2,1,0:T(8,128)(2,1)} copy(bf16[12,16,5120]{2,1,0:T(8,128)(2,1)} %get-tuple-element.8) | data formatting | bytes 3932160
  148.3 0.0 copy-done
  148.3 1.5 copy.13
Async XLA Ops:
  145.2 3.1 %copy-start = (bf16[16,16,5120]{2,1,0:T(8,128)(2,1)S(1)}, bf16[16,16,5120]{2,1,0:T(8,128)(2,1)}, u32[]{:S(2)}) copy-start(bf16[16,16,5120]{2,1,0:T(8,128)(2,1)} %get-tuple-element.5) | copy-start | bytes 7864324

commit v3 on v2

--- a/solution.py
+++ b/solution.py
@@ -11,7 +11,9 @@
 HEADS = 40
 WF = 16
 FR = 12
-AHEAD = 2
+AHEAD = 1
+VALUES_AHEAD = 2
+CHUNKS = 4
 LAG_BLEND = 1
 LAG_RETURN = 2
 LAG_LAST = 3
@@ -30,6 +32,9 @@
     kg_ref,
     owned_ref,
     next_ref,
+    q_now,
+    k_now,
+    next_out,
     stage,
     inbox,
     vbox,
@@ -62,6 +67,10 @@
     xo_recv,
     ro_send,
     ro_recv,
+    own_sem,
+    next_sem,
+    q_load,
+    k_load,
 ):
     ulysses, windows, capacity, steps, head, tokens = dims
     local = tokens // WF
@@ -73,6 +82,16 @@
 
     def far(d):
         return lax.rem(my_window + d, windows)
+
+    chunk = tokens // CHUNKS
+
+    def load(ref, now, sem, c):
+        rows = pl.ds(pl.multiple_of(c * chunk, chunk), chunk)
+        return pltpu.make_async_copy(ref.at[rows], now.at[rows], sem.at[c])
+
+    for ref, now, sem in ((q_ref, q_now, q_load), (k_ref, k_now, k_load)):
+        for c in range(CHUNKS):
+            load(ref, now, sem, c).start()
 
     barrier = pltpu.get_barrier_semaphore()
     for d in range(1, ulysses):
@@ -124,7 +143,7 @@
             "uly",
         )
 
-    for s in range(AHEAD):
+    for s in range(VALUES_AHEAD):
         send_values(s)
 
     frames_total = FR * windows
@@ -170,11 +189,19 @@
             needed = lax.rem(my_start + shift + j, windows)
             next_at[j] = owner_ref[needed] * capacity + j // windows
 
-    for which, (ref, gain) in enumerate(((q_ref, qg_ref), (k_ref, kg_ref))):
-
-        def norm_block(t, carry, which=which, ref=ref, gain=gain):
+    for which, (ref, now, sem, gain) in enumerate(
+        ((q_ref, q_now, q_load, qg_ref), (k_ref, k_now, k_load, kg_ref))
+    ):
+
+        def norm_block(t, carry, which=which, ref=ref, now=now, sem=sem, gain=gain):
+            blocks = chunk // ROWS
+
+            @pl.when(lax.rem(t, blocks) == 0)
+            def _():
+                load(ref, now, sem, t // blocks).wait()
+
             rows = pl.ds(pl.multiple_of(t * ROWS, ROWS), ROWS)
-            floats = ref[rows, :].astype(jnp.float32)
+            floats = now[rows, :].astype(jnp.float32)
             mean_square = jnp.mean(floats * floats, axis=-1, keepdims=True)
             scaled = (floats * lax.rsqrt(mean_square + 1e-06) * gain[...]).astype(jnp.bfloat16)
             for u in range(ulysses):
@@ -200,7 +227,10 @@
         def _():
             send_scored(0, s + AHEAD)
             send_scored(1, s + AHEAD)
-            send_values(s + AHEAD)
+
+        @pl.when(s + VALUES_AHEAD < steps)
+        def _():
+            send_values(s + VALUES_AHEAD)
 
         keys = inbox[1, s].reshape(ulysses * tokens, head)
         values = vbox[s].reshape(ulysses * tokens, head)
@@ -259,15 +289,19 @@
             "win",
         )
         for u in range(ulysses):
-            owned_ref[:, :, columns(u, s)] = x_in[s, u]
+            pltpu.make_async_copy(
+                x_in.at[s, u], owned_ref.at[:, :, columns(u, s)], own_sem.at[s]
+            ).start()
 
     def finish(s):
         arrived(r_in.at[s], ro_recv.at[s])
         z_now[...] = r_in[s]
         for j in range(WF):
-            frame = z_now[next_at[j]]
-            for u in range(ulysses):
-                next_ref[j, :, columns(u, s)] = frame[u]
+            next_out[s, :, j] = z_now[next_at[j]]
+        for u in range(ulysses):
+            pltpu.make_async_copy(
+                next_out.at[s, u], next_ref.at[:, :, columns(u, s)], next_sem.at[s]
+            ).start()
 
     def step(i, carry):
         for lag, work in (
@@ -292,6 +326,8 @@
         arrived(z_out.at[s, pl.ds(0, windows - 1)], zo_send.at[s])
         arrived(x_out.at[s, pl.ds(0, ulysses - 1)], xo_send.at[s])
         arrived(r_out.at[s, pl.ds(0, windows - 1)], ro_send.at[s])
+        arrived(x_in.at[s], own_sem.at[s])
+        arrived(next_out.at[s], next_sem.at[s])
         return carry
 
     lax.fori_loop(0, steps, sent, 0)
@@ -317,6 +353,7 @@
     tokens = WF * local
     smem = pl.BlockSpec(memory_space=pltpu.SMEM)
     vmem = pl.BlockSpec(memory_space=pltpu.VMEM)
+    hbm = pl.BlockSpec(memory_space=pl.ANY)
     bf16 = jnp.bfloat16
     sems = pltpu.SemaphoreType.DMA((steps,))
     frame = (ulysses, local, head)
@@ -326,9 +363,12 @@
             jax.ShapeDtypeStruct((FR, local, features), bf16),
             jax.ShapeDtypeStruct((WF, local, features), bf16),
         ),
-        in_specs=[smem] * 3 + [vmem] * 5,
-        out_specs=(vmem, vmem),
+        in_specs=[smem] * 3 + [hbm] * 3 + [vmem] * 2,
+        out_specs=(hbm, hbm),
         scratch_shapes=[
+            pltpu.VMEM((tokens, features), bf16),
+            pltpu.VMEM((tokens, features), bf16),
+            pltpu.VMEM((steps, ulysses, WF, local, head), bf16),
             pltpu.VMEM((2, ulysses, steps, tokens, head), bf16),
             pltpu.VMEM((2, steps, ulysses, tokens, head), bf16),
             pltpu.VMEM((steps, ulysses, tokens, head), bf16),
@@ -350,7 +390,8 @@
             pltpu.SMEM((windows * capacity,), jnp.int32),
             pltpu.SMEM((WF,), jnp.int32),
         ]
-        + [sems] * 12,
+        + [sems] * 14
+        + [pltpu.SemaphoreType.DMA((CHUNKS,))] * 2,
         compiler_params=pltpu.CompilerParams(
             collective_id=0, has_side_effects=True, vmem_limit_bytes=66 * 1000 * 1000
         ),

time: 150 us -> 146 us (0.973)
  Pallas kernels: 145 us -> 140 us
    pallas_call x1, Pallas kernels: 145 us -> 140 us  [per_device(): pl.pallas_call(functools.partial(fused, (ulysses, windows, capacity, step...]
where the time goes in v3:
time: 146 us; the launch traced here: 145 us
  Pallas kernels  140 us (96%)
  local copies, waits for them, and re-layouts  4.59 us (3%)
    pallas_call x1, Pallas kernels, per_device(): pl.pallas_call(functools.partial(fused, (ulysses, windows, capacity, step...  140 us
    unnamed x4, local copies, waits for them, and re-layouts  4.59 us

profile of v3, /device:TPU:0, one launch (start us, length us, event | category | flops | bytes accessed | tf_op | source)
XLA Modules:
  0.0 144.8 jit_solution(4339345498060025746)
XLA Ops:
  0.6 139.6 %shard_map.95 = (bf16[12,16,5120]{2,1,0:T(8,128)(2,1)}, bf16[16,16,5120]{2,1,0:T(8,128)(2,1)}) custom-call(s32[4]{0:T(128)} %start_ref.1, s32[4]{0:T(128)} %owner_ref.1, s32[4,16]{1,0:T(4,128)} %weight_ref.1, bf16[256,5120]{1,0:T(8,128)(2,1)} %bitcast.6, bf16[256,5120]{1,0:T(8,128)(2,1)} %bitcast.7, bf16[256,5120]{1,0:T(8,128)(2,1)} %bitcast.8, ...), custom_call_target="tpu_custom_call" | custom-call | tf_op jit(solution)/shard_map/pallas_call | solution.py:360
  140.2 0.0 copy-start
  140.2 3.1 %copy.12 = bf16[12,16,5120]{2,1,0:T(8,128)(2,1)} copy(bf16[12,16,5120]{2,1,0:T(8,128)(2,1)} %get-tuple-element.8) | data formatting | bytes 3932160
  143.3 0.0 copy-done
  143.3 1.5 %copy.13 = bf16[1,16,16,5120]{3,2,1,0:T(8,128)(2,1)} copy(bf16[1,16,16,5120]{3,2,1,0:T(8,128)(2,1)S(1)} %bitcast.9) | data formatting | bytes 5242880
Async XLA Ops:
  140.2 3.1 %copy-start = (bf16[16,16,5120]{2,1,0:T(8,128)(2,1)S(1)}, bf16[16,16,5120]{2,1,0:T(8,128)(2,1)}, u32[]{:S(2)}) copy-start(bf16[16,16,5120]{2,1,0:T(8,128)(2,1)} %get-tuple-element.5) | copy-start | bytes 7864324

commit v4 on v3

--- a/solution.py
+++ b/solution.py
@@ -11,7 +11,6 @@
 HEADS = 40
 WF = 16
 FR = 12
-AHEAD = 1
 VALUES_AHEAD = 2
 CHUNKS = 4
 LAG_BLEND = 1
@@ -35,6 +34,7 @@
     q_now,
     k_now,
     next_out,
+    root,
     stage,
     inbox,
     vbox,
@@ -125,6 +125,13 @@
     def columns(u, s):
         return pl.ds(pl.multiple_of((u * steps + s) * head, head), head)
 
+    def scale_columns(which, s):
+        now, gain = ((q_now, qg_ref), (k_now, kg_ref))[which]
+        for u in range(ulysses):
+            at = columns(u, s)
+            scaled = now[:, at].astype(jnp.float32) * root[which] * gain[:, at]
+            stage[which, u, s] = scaled.astype(jnp.bfloat16)
+
     def send_values(s):
         spread(
             lambda u: v_ref.at[:, columns(u, s)],
@@ -203,16 +210,18 @@
             rows = pl.ds(pl.multiple_of(t * ROWS, ROWS), ROWS)
             floats = now[rows, :].astype(jnp.float32)
             mean_square = jnp.mean(floats * floats, axis=-1, keepdims=True)
-            scaled = (floats * lax.rsqrt(mean_square + 1e-06) * gain[...]).astype(jnp.bfloat16)
-            for u in range(ulysses):
-                for s in range(steps):
-                    at = (u * steps + s) * head
-                    stage[which, u, s, rows, :] = scaled[:, at : at + head]
+            root[which, rows, :] = jnp.broadcast_to(
+                lax.rsqrt(mean_square + 1e-06), (ROWS, head)
+            )
             return carry
 
         lax.fori_loop(0, tokens // ROWS, norm_block, 0)
-        for s in range(AHEAD):
-            send_scored(which, s)
+        scale_columns(which, 0)
+
+    send_scored(0, 0)
+    send_scored(1, 0)
+    for which in range(2):
+        scale_columns(which, 1)
 
     tables()
 
@@ -223,10 +232,10 @@
         arrived(inbox.at[1, s], k_recv.at[s])
         arrived(vbox.at[s], v_recv.at[s])
 
-        @pl.when(s + AHEAD < steps)
+        @pl.when(s + 1 < steps)
         def _():
-            send_scored(0, s + AHEAD)
-            send_scored(1, s + AHEAD)
+            send_scored(0, s + 1)
+            send_scored(1, s + 1)
 
         @pl.when(s + VALUES_AHEAD < steps)
         def _():
@@ -260,6 +269,11 @@
             "win",
         )
 
+        @pl.when(s + 2 < steps)
+        def _():
+            for which in range(2):
+                scale_columns(which, s + 2)
+
     def blend(s):
         arrived(z_in.at[s], zo_recv.at[s])
         z_now[...] = z_in[s]
@@ -306,8 +320,8 @@
     def step(i, carry):
         for lag, work in (
             (0, attention),
+            (LAG_RETURN, give_back),
             (LAG_BLEND, blend),
-            (LAG_RETURN, give_back),
             (LAG_LAST, finish),
         ):
 
@@ -369,6 +383,7 @@
             pltpu.VMEM((tokens, features), bf16),
             pltpu.VMEM((tokens, features), bf16),
             pltpu.VMEM((steps, ulysses, WF, local, head), bf16),
+            pltpu.VMEM((2, tokens, head), jnp.float32),
             pltpu.VMEM((2, ulysses, steps, tokens, head), bf16),
             pltpu.VMEM((2, steps, ulysses, tokens, head), bf16),
             pltpu.VMEM((steps, ulysses, tokens, head), bf16),

time: 146 us -> 145 us (level)
  no operation moved by 1% of the time
where the time goes in v4:
time: 145 us
  Pallas kernels  140 us (97%)
  local copies, waits for them, and re-layouts  4.59 us (3%)
    pallas_call x1, Pallas kernels, per_device(): pl.pallas_call(functools.partial(fused, (ulysses, windows, capacity, step...  140 us
    unnamed x4, local copies, waits for them, and re-layouts  4.59 us

profile of v4, /device:TPU:0, one launch (start us, length us, event | category | flops | bytes accessed | tf_op | source)
XLA Modules:
  0.0 145.1 jit_solution(2237909567700092697)
XLA Ops:
  0.6 139.9 %shard_map.95 = (bf16[12,16,5120]{2,1,0:T(8,128)(2,1)}, bf16[16,16,5120]{2,1,0:T(8,128)(2,1)}) custom-call(s32[4]{0:T(128)} %start_ref.1, s32[4]{0:T(128)} %owner_ref.1, s32[4,16]{1,0:T(4,128)} %weight_ref.1, bf16[256,5120]{1,0:T(8,128)(2,1)} %bitcast.6, bf16[256,5120]{1,0:T(8,128)(2,1)} %bitcast.7, bf16[256,5120]{1,0:T(8,128)(2,1)} %bitcast.8, ...), custom_call_target="tpu_custom_call" | custom-call | tf_op jit(solution)/shard_map/pallas_call | solution.py:374
  140.5 0.0 copy-start
  140.5 3.1 %copy.12 = bf16[12,16,5120]{2,1,0:T(8,128)(2,1)} copy(bf16[12,16,5120]{2,1,0:T(8,128)(2,1)} %get-tuple-element.8) | data formatting | bytes 3932160
  143.6 0.0 copy-done
  143.6 1.5 %copy.13 = bf16[1,16,16,5120]{3,2,1,0:T(8,128)(2,1)} copy(bf16[1,16,16,5120]{3,2,1,0:T(8,128)(2,1)S(1)} %bitcast.9) | data formatting | bytes 5242880
Async XLA Ops:
  140.5 3.1 %copy-start = (bf16[16,16,5120]{2,1,0:T(8,128)(2,1)S(1)}, bf16[16,16,5120]{2,1,0:T(8,128)(2,1)}, u32[]{:S(2)}) copy-start(bf16[16,16,5120]{2,1,0:T(8,128)(2,1)} %get-tuple-element.5) | copy-start | bytes 7864324
